TPU v7x, 32 devices: a whole 2x2x4 slice. The times are simulated.
32 devices in a mesh: dp: 8 (over z, core), tensor: 4 (over y, x).
Axes of the slice: x: 2, y: 2, z: 4, core: 2. Of those that a mesh axis runs over, the one named last changes fastest.
Arguments:
- layer_input: bfloat16 [8192, 2048], P(('dp', 'tensor')), may hold values from -6 to 6
- norm1_gain: bfloat16 [2048], P('dp'), may hold values from 0.25 to 1.75
- norm1_bias: bfloat16 [2048], P('dp'), may hold values from -3 to 3
- qkv_weight: bfloat16 [3, 2048, 2048], P(None, 'dp', 'tensor'), may hold values from -0.125 to 0.125
- qkv_bias: bfloat16 [3, 2048], P(None, ('tensor', 'dp')), may hold values from -6 to 6
- out_weight: bfloat16 [2048, 2048], P('tensor', 'dp'), may hold values from -0.5 to 0.5
- norm2_gain: bfloat16 [2048], P('dp'), may hold values from 0.25 to 1.75
- norm2_bias: bfloat16 [2048], P('dp'), may hold values from -3 to 3
- gate_up_weight: bfloat16 [2, 2048, 5632], P(None, 'dp', 'tensor'), may hold values from -0.125 to 0.125
- down_weight: bfloat16 [5632, 2048], P('tensor', 'dp'), may hold values from -0.15625 to 0.15625
- out_cotangent: bfloat16 [8192, 2048], P(('dp', 'tensor')), may hold values from -6 to 6
Outputs:
- layer_output: bfloat16 [8192, 2048], P(('dp', 'tensor'))
- grad_input: float32 [8192, 2048], P(('dp', 'tensor'))
- grad_norm1_gain: float32 [2048], P('dp')
- grad_norm1_bias: float32 [2048], P('dp')
- grad_qkv_weight: float32 [3, 2048, 2048], P(None, 'dp', 'tensor')
- grad_qkv_bias: float32 [3, 2048], P(None, ('tensor', 'dp'))
- grad_out_weight: float32 [2048, 2048], P('tensor', 'dp')
- grad_norm2_gain: float32 [2048], P('dp')
- grad_norm2_bias: float32 [2048], P('dp')
- grad_gate_up_weight: float32 [2, 2048, 5632], P(None, 'dp', 'tensor')
- grad_down_weight: float32 [5632, 2048], P('tensor', 'dp')
All inputs are finite; a program needn't handle non-finite values.
Results may differ from a plain program's by a relative error of at most 0.025.
The roundings to bfloat16 on the way count: a program that leaves them out, or rounds other values in their place, can miss the bound.
Values may be sent and summed in bfloat16 or wider, within the bound.
No kernel may reach another device: no remote copies, remote signals or barrier semaphores. Data moves between devices by JAX's collectives and lax.ppermute only.
A program may use at most 192 MiB of HBM per device.

v0:
```python
import jax
import jax.numpy as jnp
from jax import lax
from jax.sharding import PartitionSpec as P

HEAD_DIM = 64
ROT = 16
SEQ_LEN = 512
epsilon = 1e-05


def layer_norm(values):
    row_mean = jnp.mean(values, axis=-1, keepdims=True)
    centered = values - row_mean
    inv_sigma = lax.rsqrt(jnp.mean(centered * centered, axis=-1, keepdims=True) + epsilon)
    return (centered * inv_sigma, inv_sigma)


def norm_back(grad_hat, normed, inv_sigma):
    return inv_sigma * (
        grad_hat
        - jnp.mean(grad_hat, axis=-1, keepdims=True)
        - normed * jnp.mean(grad_hat * normed, axis=-1, keepdims=True)
    )


def rotary_tables(length, rot_dims):
    half_rot = rot_dims // 2
    frequency = 10000.0 ** (-(2.0 * jnp.arange(half_rot, dtype=jnp.float32)) / rot_dims)
    angles = jnp.arange(length, dtype=jnp.float32)[:, None] * frequency[None, :]
    return (jnp.cos(angles)[:, None, :], jnp.sin(angles)[:, None, :])


def rotate(tensor, cosine_table, sine_table, rot_dims):
    half_rot = rot_dims // 2
    lower_half = tensor[..., :half_rot]
    upper_half = tensor[..., half_rot:rot_dims]
    return jnp.concatenate(
        [
            lower_half * cosine_table - upper_half * sine_table,
            upper_half * cosine_table + lower_half * sine_table,
            tensor[..., rot_dims:],
        ],
        axis=-1,
    )


def unrotate(tensor, cosine_table, sine_table, rot_dims):
    half_rot = rot_dims // 2
    lower_half = tensor[..., :half_rot]
    upper_half = tensor[..., half_rot:rot_dims]
    return jnp.concatenate(
        [
            lower_half * cosine_table + upper_half * sine_table,
            upper_half * cosine_table - lower_half * sine_table,
            tensor[..., rot_dims:],
        ],
        axis=-1,
    )


def causal_mask(length):
    places = jnp.arange(length)
    return places[:, None] >= places[None, :]


def attention_params(norm1_gain, norm1_bias, qkv_weight, qkv_bias, out_weight):
    return (
        lax.all_gather(norm1_gain, "dp", axis=0, tiled=True),
        lax.all_gather(norm1_bias, "dp", axis=0, tiled=True),
        lax.all_gather(qkv_weight, "dp", axis=1, tiled=True),
        lax.all_gather(qkv_bias, "dp", axis=1, tiled=True),
        lax.all_gather(out_weight, "dp", axis=1, tiled=True),
    )


def mlp_params(norm2_gain, norm2_bias, gate_up_weight, down_weight):
    return (
        lax.all_gather(norm2_gain, "dp", axis=0, tiled=True),
        lax.all_gather(norm2_bias, "dp", axis=0, tiled=True),
        lax.all_gather(gate_up_weight, "dp", axis=1, tiled=True),
        lax.all_gather(down_weight, "dp", axis=1, tiled=True),
    )


def collect_rows(row_block):
    return lax.all_gather(row_block, "tensor", axis=0, tiled=True)


def spread_rows(term_fn, row_total):
    return lax.psum_scatter(
        term_fn(jnp.int32(0), row_total * lax.axis_size("tensor")).astype(jnp.bfloat16),
        "tensor",
        scatter_dimension=0,
        tiled=True,
    ).astype(jnp.float32)


def shards(
    layer_input,
    norm1_gain,
    norm1_bias,
    qkv_weight,
    qkv_bias,
    out_weight,
    norm2_gain,
    norm2_bias,
    gate_up_weight,
    down_weight,
    out_cotangent,
):
    local_rows = layer_input.shape[0]
    score_scale = HEAD_DIM ** (-0.5)
    cosine_table, sine_table = rotary_tables(SEQ_LEN, ROT)
    causal = causal_mask(SEQ_LEN)
    gain_one, bias_one, qkv_local, bias_local, out_local = attention_params(
        norm1_gain, norm1_bias, qkv_weight, qkv_bias, out_weight
    )
    x_float = layer_input.astype(jnp.float32)
    hat_one, inv_one = layer_norm(x_float)
    normed_one = (hat_one * gain_one.astype(jnp.float32) + bias_one.astype(jnp.float32)).astype(
        jnp.bfloat16
    )
    rows_one = collect_rows(normed_one)
    group_rows = rows_one.shape[0]
    seq_count = group_rows // SEQ_LEN
    head_cols = qkv_local.shape[2]
    heads_here = head_cols // HEAD_DIM
    qkv_all = (
        jnp.einsum("rd,cdk->crk", rows_one, qkv_local, preferred_element_type=jnp.float32)
        + bias_local.astype(jnp.float32)[:, None, :]
    )
    qkv_all = qkv_all.reshape(3, seq_count, SEQ_LEN, heads_here, HEAD_DIM)
    query_rot = rotate(qkv_all[0], cosine_table, sine_table, ROT).astype(jnp.bfloat16)
    key_rot = rotate(qkv_all[1], cosine_table, sine_table, ROT).astype(jnp.bfloat16)
    value_heads = qkv_all[2].astype(jnp.bfloat16)

    def attend(pieces):
        query_seq, key_seq, value_seq = pieces
        scores = (
            jnp.einsum("qhd,khd->hqk", query_seq, key_seq, preferred_element_type=jnp.float32)
            * score_scale
        )
        scores = jnp.where(causal, scores, -jnp.inf)
        row_top = jnp.max(scores, axis=-1, keepdims=True)
        log_total = row_top + jnp.log(jnp.sum(jnp.exp(scores - row_top), axis=-1, keepdims=True))
        prob_low = jnp.exp(scores - log_total).astype(jnp.bfloat16)
        context_seq = jnp.einsum(
            "hqk,khd->qhd", prob_low, value_seq, preferred_element_type=jnp.float32
        ).astype(jnp.bfloat16)
        return (context_seq, log_total[..., 0])

    context, log_totals = lax.map(attend, (query_rot, key_rot, value_heads))
    context_rows = context.reshape(group_rows, head_cols)

    def attn_term(row_start, row_count):
        return jnp.dot(context_rows, out_local, preferred_element_type=jnp.float32)

    residual = x_float + spread_rows(attn_term, local_rows)
    gain_two, bias_two, gate_up_local, down_local = mlp_params(
        norm2_gain, norm2_bias, gate_up_weight, down_weight
    )
    hat_two, inv_two = layer_norm(residual)
    normed_two = (hat_two * gain_two.astype(jnp.float32) + bias_two.astype(jnp.float32)).astype(
        jnp.bfloat16
    )
    rows_two = collect_rows(normed_two)
    gate_proj = jnp.dot(rows_two, gate_up_local[0], preferred_element_type=jnp.float32)
    up_proj = jnp.dot(rows_two, gate_up_local[1], preferred_element_type=jnp.float32)
    sigmoid_gate = jax.nn.sigmoid(gate_proj)
    silu_gate = gate_proj * sigmoid_gate
    activation = (silu_gate * up_proj).astype(jnp.bfloat16)

    def mlp_term(row_start, row_count):
        return jnp.dot(activation, down_local, preferred_element_type=jnp.float32)

    layer_output = (residual + spread_rows(mlp_term, local_rows)).astype(jnp.bfloat16)
    cot_rows = collect_rows(out_cotangent)
    gain_two, bias_two, gate_up_local, down_local = mlp_params(
        norm2_gain, norm2_bias, gate_up_weight, down_weight
    )
    grad_act = lax.dot_general(
        cot_rows, down_local, (((1,), (1,)), ((), ())), preferred_element_type=jnp.float32
    )
    grad_gate = (
        grad_act * up_proj * sigmoid_gate * (1.0 + gate_proj * (1.0 - sigmoid_gate))
    ).astype(jnp.bfloat16)
    grad_up = (grad_act * silu_gate).astype(jnp.bfloat16)
    grad_down = lax.dot_general(
        activation, cot_rows, (((0,), (0,)), ((), ())), preferred_element_type=jnp.float32
    )
    grad_wgate = lax.dot_general(
        rows_two, grad_gate, (((0,), (0,)), ((), ())), preferred_element_type=jnp.float32
    )
    grad_wup = lax.dot_general(
        rows_two, grad_up, (((0,), (0,)), ((), ())), preferred_element_type=jnp.float32
    )

    def mlp_back_term(row_start, row_count):
        gate_back = lax.dot_general(
            grad_gate,
            gate_up_local[0],
            (((1,), (1,)), ((), ())),
            preferred_element_type=jnp.float32,
        )
        up_back = lax.dot_general(
            grad_up, gate_up_local[1], (((1,), (1,)), ((), ())), preferred_element_type=jnp.float32
        )
        return gate_back + up_back

    grad_normed_two = spread_rows(mlp_back_term, local_rows)
    grad_gain_two = jnp.sum(grad_normed_two * hat_two, axis=0)
    grad_bias_two = jnp.sum(grad_normed_two, axis=0)
    grad_resid = out_cotangent.astype(jnp.float32) + norm_back(
        grad_normed_two * gain_two.astype(jnp.float32), hat_two, inv_two
    )
    mlp_shares = (
        lax.psum_scatter(
            grad_wgate.astype(jnp.bfloat16), "dp", scatter_dimension=0, tiled=True
        ).astype(jnp.float32),
        lax.psum_scatter(
            grad_wup.astype(jnp.bfloat16), "dp", scatter_dimension=0, tiled=True
        ).astype(jnp.float32),
        lax.psum_scatter(
            grad_down.astype(jnp.bfloat16), "dp", scatter_dimension=1, tiled=True
        ).astype(jnp.float32),
        lax.psum_scatter(
            grad_gain_two.astype(jnp.bfloat16), "dp", scatter_dimension=0, tiled=True
        ).astype(jnp.float32),
        lax.psum_scatter(
            grad_bias_two.astype(jnp.bfloat16), "dp", scatter_dimension=0, tiled=True
        ).astype(jnp.float32),
    )
    grad_resid_rows = collect_rows(grad_resid.astype(jnp.bfloat16))
    gain_one, bias_one, qkv_local, bias_local, out_local = attention_params(
        norm1_gain, norm1_bias, qkv_weight, qkv_bias, out_weight
    )
    grad_context = lax.dot_general(
        grad_resid_rows, out_local, (((1,), (1,)), ((), ())), preferred_element_type=jnp.float32
    ).astype(jnp.bfloat16)
    grad_wout = lax.dot_general(
        context_rows, grad_resid_rows, (((0,), (0,)), ((), ())), preferred_element_type=jnp.float32
    )
    grad_ctx_heads = grad_context.reshape(seq_count, SEQ_LEN, heads_here, HEAD_DIM)

    def attend_back(pieces):
        query_seq, key_seq, value_seq, context_seq, grad_ctx_seq, total_seq = pieces
        scores = (
            jnp.einsum("qhd,khd->hqk", query_seq, key_seq, preferred_element_type=jnp.float32)
            * score_scale
        )
        scores = jnp.where(causal, scores, -jnp.inf)
        prob_full = jnp.exp(scores - total_seq[..., None])
        prob_low = prob_full.astype(jnp.bfloat16)
        grad_probs = jnp.einsum(
            "qhd,khd->hqk", grad_ctx_seq, value_seq, preferred_element_type=jnp.float32
        )
        delta_sum = jnp.einsum(
            "qhd,qhd->hq", grad_ctx_seq, context_seq, preferred_element_type=jnp.float32
        )
        grad_scores = (prob_full * (grad_probs - delta_sum[..., None]) * score_scale).astype(
            jnp.bfloat16
        )
        grad_value_seq = jnp.einsum(
            "hqk,qhd->khd", prob_low, grad_ctx_seq, preferred_element_type=jnp.float32
        )
        grad_query_seq = jnp.einsum(
            "hqk,khd->qhd", grad_scores, key_seq, preferred_element_type=jnp.float32
        )
        grad_key_seq = jnp.einsum(
            "hqk,qhd->khd", grad_scores, query_seq, preferred_element_type=jnp.float32
        )
        return (grad_query_seq, grad_key_seq, grad_value_seq)

    grad_query, grad_keys, grad_values = lax.map(
        attend_back, (query_rot, key_rot, value_heads, context, grad_ctx_heads, log_totals)
    )
    grad_query = unrotate(grad_query, cosine_table, sine_table, ROT)
    grad_keys = unrotate(grad_keys, cosine_table, sine_table, ROT)
    grad_pre = (
        jnp.stack([grad_query, grad_keys, grad_values])
        .astype(jnp.bfloat16)
        .reshape(3, group_rows, head_cols)
    )
    grad_bqkv = jnp.sum(grad_pre, axis=1, dtype=jnp.float32)
    grad_wqkv = jnp.einsum("rd,crk->cdk", rows_one, grad_pre, preferred_element_type=jnp.float32)

    def qkv_back_term(row_start, row_count):
        return jnp.einsum("crk,cdk->rd", grad_pre, qkv_local, preferred_element_type=jnp.float32)

    grad_normed_one = spread_rows(qkv_back_term, local_rows)
    grad_gain_one = jnp.sum(grad_normed_one * hat_one, axis=0)
    grad_bias_one = jnp.sum(grad_normed_one, axis=0)
    grad_input = grad_resid + norm_back(
        grad_normed_one * gain_one.astype(jnp.float32), hat_one, inv_one
    )
    attn_shares = (
        lax.psum_scatter(
            grad_wqkv.astype(jnp.bfloat16), "dp", scatter_dimension=1, tiled=True
        ).astype(jnp.float32),
        lax.psum_scatter(
            grad_bqkv.astype(jnp.bfloat16), "dp", scatter_dimension=1, tiled=True
        ).astype(jnp.float32),
        lax.psum_scatter(
            grad_wout.astype(jnp.bfloat16), "dp", scatter_dimension=1, tiled=True
        ).astype(jnp.float32),
        lax.psum_scatter(
            grad_gain_one.astype(jnp.bfloat16), "dp", scatter_dimension=0, tiled=True
        ).astype(jnp.float32),
        lax.psum_scatter(
            grad_bias_one.astype(jnp.bfloat16), "dp", scatter_dimension=0, tiled=True
        ).astype(jnp.float32),
    )
    norm_totals = lax.psum((attn_shares[3], attn_shares[4], mlp_shares[3], mlp_shares[4]), "tensor")
    grad_gate_up = jnp.stack([mlp_shares[0], mlp_shares[1]])
    return (
        layer_output,
        grad_input,
        norm_totals[0],
        norm_totals[1],
        attn_shares[0],
        attn_shares[1],
        attn_shares[2],
        norm_totals[2],
        norm_totals[3],
        grad_gate_up,
        mlp_shares[2],
    )


def solution(mesh):
    placed = (
        P(("dp", "tensor"), None),
        P("dp"),
        P("dp"),
        P(None, "dp", "tensor"),
        P(None, ("tensor", "dp")),
        P("tensor", "dp"),
        P("dp"),
        P("dp"),
        P(None, "dp", "tensor"),
        P("tensor", "dp"),
        P(("dp", "tensor"), None),
    )
    return jax.shard_map(
        shards,
        mesh=mesh,
        in_specs=placed,
        out_specs=(
            P(("dp", "tensor"), None),
            P(("dp", "tensor"), None),
            P("dp"),
            P("dp"),
            P(None, "dp", "tensor"),
            P(None, ("tensor", "dp")),
            P("tensor", "dp"),
            P("dp"),
            P("dp"),
            P(None, "dp", "tensor"),
            P("tensor", "dp"),
        ),
        check_vma=False,
    )
```

profile of v0, /device:TPU:0, one launch (start us, length us, event | category | flops | bytes accessed | tf_op | source)
XLA Modules:
  0.0 1152.0 jit_solution(1779346989243993215)
XLA Ops:
  11.1 13.5 %all-gather = bf16[8,1,256]{2,1,0:T(2,128)(2,1)S(1)} all-gather(bf16[1,1,256]{2,1,0:T(2,128)(2,1)S(1)} %reshape.169), channel_id=1, replica_groups=mesh['dp'=8,'tensor'=4] {'dp'}, dimensions={0}, use_global_device_ids=true | all-gather | bytes 4608 | tf_op jit(solution)/shard_map/all_gather | solution.py:69
  37.1 10.1 all-gather.2
  47.4 40.1 %all-gather.14.cloned.1.call-done = bf16[1024,2048]{1,0:T(8,128)(2,1)} async-done(((bf16[256,2048]{1,0:T(8,128)(2,1)}), bf16[1024,2048]{1,0:T(8,128)(2,1)}) %all-gather.14.cloned.1.call-update) | async-done | bytes 4194320 | tf_op jit(solution)/shard_map/all_gather | solution.py:87
  87.6 66.3 %all-gather.16.cloned.1.call-done = bf16[3,2048,512]{2,1,0:T(8,128)(2,1)} async-done(((bf16[3,256,512]{2,1,0:T(8,128)(2,1)}), bf16[3,2048,512]{2,1,0:T(8,128)(2,1)}) %all-gather.16.cloned.1.call-update) | async-done | bytes 6291472 | tf_op jit(solution)/shard_map/all_gather | solution.py:71
  153.9 10.2 add_bitcast_fusion
  193.2 13.7 %while.28 = (s32[]{:T(128)}, bf16[2,512,8,64]{1,3,2,0:T(8,128)(2,1)}, f32[2,8,512]{2,1,0:T(8,128)S(1)}, bf16[2,512,8,64]{1,3,2,0:T(8,128)(2,1)}, bf16[2,512,8,64...) while((s32[]{:T(128)}, bf16[2,512,8,64]{1,3,2,0:T(8,128)(2,1)}, ...), condition=%wide.region_5.6_spmd.clone, body=%wide.region_2.5_spmd.clone.sunk | while | flops 560459776 | bytes 41027748 | solution.py:153
  226.7 9.7 all-gather.4
  236.4 31.8 %reduce-scatter.13.cloned.1.call-done = bf16[256,2048]{1,0:T(8,128)(2,1)} async-done(((bf16[1024,2048]{1,0:T(8,128)(2,1)}), bf16[256,2048]{1,0:T(8,128)(2,1)}) %reduce-scatter.13.cloned.1.call-update) | async-done | bytes 1048592 | tf_op jit(solution)/shard_map/reduce_scatter | solution.py:91
  274.7 103.0 %all-gather.22.cloned.1.call-done = bf16[2,2048,1408]{2,1,0:T(8,128)(2,1)} async-done(((bf16[2,256,1408]{2,1,0:T(8,128)(2,1)}), bf16[2,2048,1408]{2,1,0:T(8,128)(2,1)}) %all-gather.22.cloned.1.call-update) | async-done | bytes 11534352 | tf_op jit(solution)/shard_map/all_gather | solution.py:81
  377.7 53.1 %all-gather.20.cloned.1.call-done = bf16[1024,2048]{1,0:T(8,128)(2,1)} async-done(((bf16[256,2048]{1,0:T(8,128)(2,1)}), bf16[1024,2048]{1,0:T(8,128)(2,1)}) %all-gather.20.cloned.1.call-update) | async-done | bytes 4194320 | tf_op jit(solution)/shard_map/all_gather | solution.py:87
  430.9 12.2 %fusion.57 = f32[1024,1408]{1,0:T(8,128)} fusion(bf16[1024,2048]{1,0:T(8,128)(2,1)} %all-gather.20.cloned.1.call-done, bf16[2,2048,1408]{2,1,0:T(8,128)(2,1)} %all-gather.22.cloned.1.call-done), kind=kOutput, calls=%fused_computation.78 | convolution fusion | flops 5905580032 | bytes 15728640 | tf_op jit(solution)/shard_map/dot_general | solution.py:168
  451.5 33.8 %all-gather.26.cloned.1.call-done = bf16[1024,2048]{1,0:T(8,128)(2,1)} async-done(((bf16[256,2048]{1,0:T(8,128)(2,1)}), bf16[1024,2048]{1,0:T(8,128)(2,1)}) %all-gather.26.cloned.1.call-update) | async-done | bytes 4194320 | tf_op jit(solution)/shard_map/all_gather | solution.py:87
  485.3 62.4 %all-gather.24.cloned.1.call-done = bf16[1408,2048]{1,0:T(8,128)(2,1)} async-done(((bf16[1408,256]{1,0:T(8,128)(2,1)}), bf16[1408,2048]{1,0:T(8,128)(2,1)}) %all-gather.24.cloned.1.call-update) | async-done | bytes 5767184 | tf_op jit(solution)/shard_map/all_gather | solution.py:82
  547.8 16.7 %multiply_convert_fusion.1 = (bf16[1024,1408]{1,0:T(8,128)(2,1)}, bf16[1024,1408]{1,0:T(8,128)(2,1)}, bf16[1024,1408]{1,0:T(8,128)(2,1)}) fusion(f32[1024,1408]{1,0:T(8,128)} %fusion.57, f32[1024,1408]{1,0:T(8,128)} %fusion.59, bf16[1024,2048]{1,0:T(8,128)(2,1)} %all-gather.26.cloned.1.call-done, bf16[1408,2048]{1,0:T(8,128)(2,1)} %all-gather.24.cloned.1.call-done), kind=kOutput, calls=%fused_computation.72 | convolution fusion | flops 5927206912 | bytes 30146560 | tf_op jit(solution)/shard_map/dot_general | solution.py:182
  564.4 9.7 fusion.56
  574.2 10.2 add_convert_fusion
  584.8 50.5 %reduce-scatter.17.cloned.1.call-done = bf16[256,2048]{1,0:T(8,128)(2,1)} async-done(((bf16[1024,2048]{1,0:T(8,128)(2,1)}), bf16[256,2048]{1,0:T(8,128)(2,1)}) %reduce-scatter.17.cloned.1.call-update) | async-done | bytes 1048592 | tf_op jit(solution)/shard_map/reduce_scatter | solution.py:91
  641.0 10.5 convolution_convert_fusion
  651.6 11.0 convolution_convert_fusion.2
  662.7 11.0 convolution_convert_fusion.1
  673.7 20.0 %all-gather.28.cloned.1.call-done = bf16[1024,2048]{1,0:T(8,128)(2,1)} async-done(((bf16[256,2048]{1,0:T(8,128)(2,1)}), bf16[1024,2048]{1,0:T(8,128)(2,1)}) %all-gather.28.cloned.1.call-update) | async-done | bytes 4194320 | tf_op jit(solution)/shard_map/all_gather | solution.py:87
  704.8 44.3 %while.29 = (s32[]{:T(128)}, f32[2,512,8,64]{1,3,2,0:T(8,128)}, f32[2,512,8,64]{1,3,2,0:T(8,128)}, bf16[2,512,8,64]{1,3,2,0:T(8,128)(2,1)}, bf16[2,512,8,64]{1,3...) while((s32[]{:T(128)}, f32[2,512,8,64]{1,3,2,0:T(8,128)}, ...), condition=%wide.region_14.15_spmd.clone, body=%wide.region_13.14_spmd.clone.sunk | while | flops 1366552576 | bytes 111810008 | solution.py:275
  786.0 11.2 bitcast_convert_fusion.1
  797.2 11.0 convolution_convert_fusion.3
  808.3 11.6 %convert_bitcast_fusion = bf16[3,2048,512]{1,2,0:T(8,128)(2,1)} fusion(bf16[3,1024,512]{2,1,0:T(8,128)(2,1)} %constant_dynamic-update-slice_fusion, bf16[1024,2048]{1,0:T(8,128)(2,1)} %all-gather.14.cloned.1.call-done), kind=kOutput, calls=%fused_computation.68 | convolution fusion | flops 6445596672 | bytes 13631488 | tf_op jit(solution)/shard_map/rd,crk->cdk/dot_general | solution.py:286
  826.2 65.6 %reduce-scatter.27.cloned.1.call-done = bf16[256,1408]{1,0:T(8,128)(2,1)} async-done(((bf16[2048,1408]{1,0:T(8,128)(2,1)}), bf16[256,1408]{1,0:T(8,128)(2,1)}) %reduce-scatter.27.cloned.1.call-update) | async-done | bytes 720912 | tf_op jit(solution)/shard_map/reduce_scatter | solution.py:221
  895.0 28.5 %reduce-scatter.31.cloned.1.call-done = bf16[64,3]{1,0:T(8,128)(2,1)} async-done(((bf16[512,3]{1,0:T(8,128)(2,1)}), bf16[64,3]{1,0:T(8,128)(2,1)}) %reduce-scatter.31.cloned.1.call-update) | async-done | bytes 400
  924.9 35.7 %reduce-scatter.23.cloned.1.call-done = bf16[512,256]{1,0:T(8,128)(2,1)} async-done(((bf16[512,2048]{1,0:T(8,128)(2,1)}), bf16[512,256]{1,0:T(8,128)(2,1)}) %reduce-scatter.23.cloned.1.call-update) | async-done | bytes 262160 | tf_op jit(solution)/shard_map/reduce_scatter | solution.py:304
  962.4 52.2 %reduce-scatter.19.cloned.1.call-done = bf16[256,2048]{1,0:T(8,128)(2,1)} async-done(((bf16[1024,2048]{1,0:T(8,128)(2,1)}), bf16[256,2048]{1,0:T(8,128)(2,1)}) %reduce-scatter.19.cloned.1.call-update) | async-done | bytes 1048592 | tf_op jit(solution)/shard_map/reduce_scatter | solution.py:91
  1018.2 28.4 %all-reduce.5 = (bf16[2048]{0:T(1024)(128)(2,1)S(1)}, bf16[2048]{0:T(1024)(128)(2,1)S(1)}, bf16[2048]{0:T(1024)(128)(2,1)S(1)}, bf16[2048]{0:T(1024)(128)(2,1)S(1)}) all-reduce(bf16[2048]{0:T(1024)(128)(2,1)S(1)} %get-tuple-element.259, bf16[2048]{0:T(1024)(128)(2,1)S(1)} %reduce_sum.144, ...), channel_id=6, replica_groups=mesh['dp'=8,'tensor'=4] {'dp'}, use_global_device_ids=true, to_apply=%region_19.20.clone | all-reduce | flops 8192 | bytes 32768
  1056.4 13.8 %reduce-scatter.15.cloned.1.call-done = bf16[256,2048]{1,0:T(8,128)(2,1)} async-done(((bf16[1024,2048]{1,0:T(8,128)(2,1)}), bf16[256,2048]{1,0:T(8,128)(2,1)}) %reduce-scatter.15.cloned.1.call-update) | async-done | bytes 1048592 | tf_op jit(solution)/shard_map/reduce_scatter | solution.py:91
  1075.0 67.2 %reduce-scatter.21.cloned.1.call-done = bf16[3,256,512]{1,2,0:T(8,128)(2,1)} async-done(((bf16[3,2048,512]{1,2,0:T(8,128)(2,1)}), bf16[3,256,512]{1,2,0:T(8,128)(2,1)}) %reduce-scatter.21.cloned.1.call-update) | async-done | bytes 786448 | tf_op jit(solution)/shard_map/reduce_scatter | solution.py:298
  (313 shorter events, 224.2 us)
Async XLA Ops:
  7.2 80.4 %all-gather.14.cloned.1.call-start = ((), (), s32[]{:S(2)}) async-start(), calls=%async_computation.10 | async-start | bytes 5242880 | tf_op jit(solution)/shard_map/all_gather | solution.py:87
  35.5 118.4 %all-gather.16.cloned.1.call-start = ((), (), s32[]{:S(2)}) async-start(), calls=%async_computation.11 | async-start | bytes 7077888 | tf_op jit(solution)/shard_map/all_gather | solution.py:71
  36.3 174.2 %all-gather.18.cloned.1.call-start = ((), (), s32[]{:S(2)}) async-start(), calls=%async_computation.12 | async-start | bytes 2359296 | tf_op jit(solution)/shard_map/all_gather | solution.py:73
  37.0 231.2 %reduce-scatter.13.cloned.1.call-start = ((), (), s32[]{:S(2)}) async-start(), calls=%async_computation.13 | async-start | bytes 5242880 | tf_op jit(solution)/shard_map/reduce_scatter | solution.py:91
  47.4 133.6 %copy-start.28 = (f32[512,8]{0,1:T(8,128)}, f32[512,8]{0,1:T(8,128)S(1)}, u32[]{:S(2)}) copy-start(f32[512,8]{0,1:T(8,128)S(1)} %get-tuple-element.326) | copy-start | bytes 49156
  47.4 133.6 %copy-start.30 = (f32[512,8]{0,1:T(8,128)}, f32[512,8]{0,1:T(8,128)S(1)}, u32[]{:S(2)}) copy-start(f32[512,8]{0,1:T(8,128)S(1)} %get-tuple-element.327) | copy-start | bytes 49156
  216.8 160.9 %all-gather.22.cloned.1.call-start = ((), (), s32[]{:S(2)}) async-start(), calls=%async_computation.15 | async-start | bytes 12976128 | tf_op jit(solution)/shard_map/all_gather | solution.py:81
  217.4 213.5 %all-gather.20.cloned.1.call-start = ((), (), s32[]{:S(2)}) async-start(), calls=%async_computation.14 | async-start | bytes 5242880 | tf_op jit(solution)/shard_map/all_gather | solution.py:87
  226.6 412.0 %copy-start.26 = (f32[8,1,256]{2,1,0:T(1,128)}, f32[8,1,256]{2,1,0:T(1,128)S(1)}, u32[]{:S(2)}) copy-start(f32[8,1,256]{2,1,0:T(1,128)S(1)} %convert_element_type.191) | copy-start | bytes 24580
  269.9 368.8 %copy-start.34 = (f32[256]{0:T(256)}, f32[256]{0:T(256)S(1)}, u32[]{:S(2)}) copy-start(f32[256]{0:T(256)S(1)} %broadcast_multiply_fusion.4) | copy-start | bytes 3076
  271.6 367.1 %copy-start.38 = (f32[256]{0:T(256)}, f32[256]{0:T(256)S(1)}, u32[]{:S(2)}) copy-start(f32[256]{0:T(256)S(1)} %add_rsqrt_fusion) | copy-start | bytes 3076
  273.2 212.1 %all-gather.26.cloned.1.call-start = ((), (), s32[]{:S(2)}) async-start(), calls=%async_computation.18 | async-start | bytes 5242880 | tf_op jit(solution)/shard_map/all_gather | solution.py:87
  273.9 273.8 %all-gather.24.cloned.1.call-start = ((), (), s32[]{:S(2)}) async-start(), calls=%async_computation.16 | async-start | bytes 6488064 | tf_op jit(solution)/shard_map/all_gather | solution.py:82
  274.7 360.6 %reduce-scatter.17.cloned.1.call-start = ((), (), s32[]{:S(2)}) async-start(), calls=%async_computation.19 | async-start | bytes 5242880 | tf_op jit(solution)/shard_map/reduce_scatter | solution.py:91
  584.4 109.3 %all-gather.28.cloned.1.call-start = ((), (), s32[]{:S(2)}) async-start(), calls=%async_computation.20 | async-start | bytes 5242880 | tf_op jit(solution)/shard_map/all_gather | solution.py:87
  641.0 181.0 %reduce-scatter.29.cloned.1.call-start = ((), (), s32[]{:S(2)}) async-start(), calls=%async_computation.26 | async-start | bytes 6488064 | tf_op jit(solution)/shard_map/reduce_scatter | solution.py:224
  651.6 174.7 %reduce-scatter.25.cloned.1.call-start = ((), (), s32[]{:S(2)}) async-start(), calls=%async_computation.24 | async-start | bytes 6488064 | tf_op jit(solution)/shard_map/reduce_scatter | solution.py:218
  662.6 229.2 %reduce-scatter.27.cloned.1.call-start = ((), (), s32[]{:S(2)}) async-start(), calls=%async_computation.25 | async-start | bytes 6488064 | tf_op jit(solution)/shard_map/reduce_scatter | solution.py:221
  673.6 249.9 %reduce-scatter.31.cloned.1.call-start = ((), (), s32[]{:S(2)}) async-start(), calls=%async_computation.27 | async-start | bytes 147456
  779.9 180.7 %reduce-scatter.23.cloned.1.call-start = ((), (), s32[]{:S(2)}) async-start(), calls=%async_computation.23 | async-start | bytes 2359296 | tf_op jit(solution)/shard_map/reduce_scatter | solution.py:304
  785.9 228.7 %reduce-scatter.19.cloned.1.call-start = ((), (), s32[]{:S(2)}) async-start(), calls=%async_computation.21 | async-start | bytes 5242880 | tf_op jit(solution)/shard_map/reduce_scatter | solution.py:91
  797.2 273.0 %reduce-scatter.15.cloned.1.call-start = ((), (), s32[]{:S(2)}) async-start(), calls=%async_computation.17 | async-start | bytes 5242880 | tf_op jit(solution)/shard_map/reduce_scatter | solution.py:91
  808.2 333.9 %reduce-scatter.21.cloned.1.call-start = ((), (), s32[]{:S(2)}) async-start(), calls=%async_computation.22 | async-start | bytes 7077888 | tf_op jit(solution)/shard_map/reduce_scatter | solution.py:298
  891.8 124.2 %copy-start.33 = (f32[8,1,256]{2,1,0:T(1,128)S(1)}, f32[8,1,256]{2,1,0:T(1,128)}, u32[]{:S(2)}) copy-start(f32[8,1,256]{2,1,0:T(1,128)} %copy-done.32) | copy-start | bytes 24580
  891.8 124.2 %copy-start.37 = (f32[256]{0:T(256)S(1)}, f32[256]{0:T(256)}, u32[]{:S(2)}) copy-start(f32[256]{0:T(256)} %copy-done.36) | copy-start | bytes 3076
  891.8 124.2 %copy-start.42 = (f32[256]{0:T(256)S(1)}, f32[256]{0:T(256)}, u32[]{:S(2)}) copy-start(f32[256]{0:T(256)} %copy-done.41) | copy-start | bytes 3076
  895.0 175.2 %copy-start.8 = (bf16[256,2048]{1,0:T(8,128)(2,1)S(1)}, bf16[256,2048]{1,0:T(8,128)(2,1)}, u32[]{:S(2)}) copy-start(bf16[256,2048]{1,0:T(8,128)(2,1)} %reduce-scatter.13.cloned.1.call-done) | copy-start | bytes 3145732
  895.0 175.2 %copy-start.27 = (f32[8,1,256]{2,1,0:T(1,128)S(1)}, f32[8,1,256]{2,1,0:T(1,128)}, u32[]{:S(2)}) copy-start(f32[8,1,256]{2,1,0:T(1,128)} %copy-done.26) | copy-start | bytes 24580
  895.0 175.2 %copy-start.35 = (f32[256]{0:T(256)S(1)}, f32[256]{0:T(256)}, u32[]{:S(2)}) copy-start(f32[256]{0:T(256)} %copy-done.34) | copy-start | bytes 3076
  895.0 175.2 %copy-start.39 = (f32[256]{0:T(256)S(1)}, f32[256]{0:T(256)}, u32[]{:S(2)}) copy-start(f32[256]{0:T(256)} %copy-done.38) | copy-start | bytes 3076
  895.0 175.2 %copy-start.44 = (f32[256]{0:T(256)S(1)}, f32[256]{0:T(256)}, u32[]{:S(2)}) copy-start(f32[256]{0:T(256)} %copy-done.43) | copy-start | bytes 3076
  895.0 175.2 %copy-start.46 = (f32[256]{0:T(256)S(1)}, f32[256]{0:T(256)}, u32[]{:S(2)}) copy-start(f32[256]{0:T(256)} %copy-done.45) | copy-start | bytes 3076
  (57 other events, 566.7 us)
Sparse Core Ops, SparseCore 0:
  35.6 51.8 all-gather.13
  89.2 64.6 all-gather.15
  155.5 29.2 all-gather.17
  216.9 51.2 reduce-scatter.12
  269.6 108.0 all-gather.21
  380.0 50.8 all-gather.19
  432.7 52.5 all-gather.25
  486.9 60.7 all-gather.23
  584.5 50.8 reduce-scatter.16
  641.1 52.5 all-gather.27
  696.0 64.7 reduce-scatter.28
  763.0 63.2 reduce-scatter.24
  828.5 63.2 reduce-scatter.26
  894.5 29.0 reduce-scatter.30
  926.3 34.3 reduce-scatter.22
  963.5 51.0 reduce-scatter.18
  1017.4 52.7 reduce-scatter.14
  1072.4 69.7 reduce-scatter.20
where the time goes:
time: 1160 us; the launch traced here: 1150 us
  waiting for transfers between devices  730 us (63%)
  matrix products  182 us (16%)
  blocking collectives  89 us (8%)
  local copies, waits for them, and re-layouts  84.5 us (7%)
  other arithmetic  49.1 us (4%)
  between operations  16.1 us (1%)
    reduce_scatter x4, waiting for transfers between devices, spread_rows(): lax.psum_scatter(term_fn(jnp.int32(0), row_total * lax.axis_size('tensor'...  148 us
    all_gather x4, waiting for transfers between devices, collect_rows(): return lax.all_gather(row_block, 'tensor', axis=0, tiled=True)  147 us
    all_gather x1, waiting for transfers between devices, mlp_params(): lax.all_gather(gate_up_weight, 'dp', axis=1, tiled=True)  103 us
    reduce_scatter x1, waiting for transfers between devices, shards(): lax.psum_scatter(grad_wqkv.astype(jnp.bfloat16), 'dp', scatter_dimension=...  67.2 us
    all_gather x1, waiting for transfers between devices, attention_params(): lax.all_gather(qkv_weight, 'dp', axis=1, tiled=True)  66.3 us
    reduce_scatter x1, waiting for transfers between devices, shards(): lax.psum_scatter(grad_wup.astype(jnp.bfloat16), 'dp', scatter_dimension=0...  65.6 us
    all_gather x1, waiting for transfers between devices, mlp_params(): lax.all_gather(down_weight, 'dp', axis=1, tiled=True)  62.4 us
    reduce_scatter x1, waiting for transfers between devices, shards(): lax.psum_scatter(grad_wout.astype(jnp.bfloat16), 'dp', scatter_dimension=...  35.7 us
  transfers between devices with their start and end apart: 18, of which 16 were waited for; matrix products, arithmetic and copies ran while one was open for 22% of the time, Pallas kernels for 0%

commit v1 on v0

--- a/solution.py
+++ b/solution.py
@@ -84,7 +84,28 @@
 
 
 def collect_rows(row_block):
-    return lax.all_gather(row_block, "tensor", axis=0, tiled=True)
+
+    def search_the_row(field):
+        response, q_next, piece_out = (
+            jax.lax.axis_size("tensor"),
+            jax.lax.axis_index("tensor"),
+            field.shape[0],
+        )
+        b_now, w2 = (field, 1)
+        while w2 < response:
+            b_now = jnp.concatenate(
+                [
+                    b_now,
+                    jax.lax.ppermute(
+                        b_now, "tensor", [(j0, (j0 - w2) % response) for j0 in range(response)]
+                    ),
+                ],
+                0,
+            )
+            w2 = 2 * w2
+        return jnp.roll(b_now, shift=q_next * piece_out, axis=0)
+
+    return search_the_row(row_block)
 
 
 def spread_rows(term_fn, row_total):

time: 1160 us -> 982 us (0.85)
  waiting for transfers between devices: 730 us -> 492 us
  other arithmetic: 49.1 us -> 97.7 us
  starting transfers between devices: 1.13 us -> 15.3 us
    ppermute x0 -> x8, waiting for transfers between devices: none -> 206 us  [search_the_row(): jax.lax.ppermute(b_now, 'tensor', [(j0, (j0 - w2) % response) for j0 in r...]
    all_gather x4 -> x0, waiting for transfers between devices: 147 us -> none  [collect_rows(): return lax.all_gather(row_block, 'tensor', axis=0, tiled=True)]
    all_gather x1, waiting for transfers between devices: 103 us -> 0.01 us  [mlp_params(): lax.all_gather(gate_up_weight, 'dp', axis=1, tiled=True)]
    all_gather x1, waiting for transfers between devices: 66.3 us -> 0.01 us  [attention_params(): lax.all_gather(qkv_weight, 'dp', axis=1, tiled=True)]
    reduce_scatter x1, waiting for transfers between devices: 65.6 us -> 0.02 us  [shards(): lax.psum_scatter(grad_wup.astype(jnp.bfloat16), 'dp', scatter_dimension=0...]
    concatenate x0 -> x6, other arithmetic: none -> 40.1 us  [the longest x2 34 us: search_the_row(): return jnp.roll(b_now, shift=q_next * piece_out, axis=0)]
    all_gather x1, waiting for transfers between devices: 62.4 us -> 27.3 us  [mlp_params(): lax.all_gather(down_weight, 'dp', axis=1, tiled=True)]
    unnamed x19 -> x15, waiting for transfers between devices: 32 us -> 14 us
  transfers between devices with their start and end apart: 18 -> 22, of which waited for: 16 -> 15; matrix products, arithmetic and copies ran while one was open for 22% -> 31% of each run, Pallas kernels for 0% -> 0%
where the time goes in v1:
time: 982 us; the launch traced here: 971 us
  waiting for transfers between devices  492 us (50%)
  matrix products  175 us (18%)
  other arithmetic  97.7 us (10%)
  blocking collectives  91.7 us (9%)
  local copies, waits for them, and re-layouts  82.6 us (8%)
  between operations  15.6 us (2%)
  starting transfers between devices  15.3 us (2%)
    ppermute x8, waiting for transfers between devices, search_the_row(): jax.lax.ppermute(b_now, 'tensor', [(j0, (j0 - w2) % response) for j0 in r...  206 us
    reduce_scatter x4, waiting for transfers between devices, spread_rows(): lax.psum_scatter(term_fn(jnp.int32(0), row_total * lax.axis_size('tensor'...  142 us
    reduce_scatter x1, waiting for transfers between devices, shards(): lax.psum_scatter(grad_wqkv.astype(jnp.bfloat16), 'dp', scatter_dimension=...  67.2 us
    reduce_scatter x1, waiting for transfers between devices, shards(): lax.psum_scatter(grad_wout.astype(jnp.bfloat16), 'dp', scatter_dimension=...  35.7 us
    concatenate x2, other arithmetic, search_the_row(): return jnp.roll(b_now, shift=q_next * piece_out, axis=0)  34 us
    unnamed x1, blocking collectives  28.4 us
    all_gather x1, waiting for transfers between devices, mlp_params(): lax.all_gather(down_weight, 'dp', axis=1, tiled=True)  27.3 us
  transfers between devices with their start and end apart: 22, of which 15 were waited for; matrix products, arithmetic and copies ran while one was open for 31% of the time, Pallas kernels for 0%

profile of v1, /device:TPU:0, one launch (start us, length us, event | category | flops | bytes accessed | tf_op | source)
XLA Modules:
  0.0 970.9 jit_solution(367154697382319040)
XLA Ops:
  8.6 13.5 %all-gather = bf16[8,1,256]{2,1,0:T(2,128)(2,1)S(1)} all-gather(bf16[1,1,256]{2,1,0:T(2,128)(2,1)S(1)} %reshape.169), channel_id=1, replica_groups=mesh['dp'=8,'tensor'=4] {'dp'}, dimensions={0}, use_global_device_ids=true | all-gather | bytes 4608 | tf_op jit(solution)/shard_map/all_gather | solution.py:69
  39.4 23.0 %collective-permute-done = bf16[256,2048]{1,0:T(8,128)(2,1)S(1)} collective-permute-done((bf16[256,2048]{1,0:T(8,128)(2,1)S(1)}, bf16[256,2048]{1,0:T(8,128)(2,1)S(1)}, u32[]{:S(2)}, u32[]{:S(2)}) %collective-permute-start) | collective-permute-done | bytes 1048608 | tf_op jit(solution)/shard_map/ppermute | solution.py:99
  65.4 11.4 %all-gather.2 = bf16[8,64,3]{1,2,0:T(4,128)(2,1)S(1)} all-gather(bf16[1,64,3]{1,2,0:T(4,128)(2,1)S(1)} %bitcast.199), channel_id=1, replica_groups=mesh['dp'=8,'tensor'=4] {'dp'}, dimensions={0}, use_global_device_ids=true | all-gather | bytes 3456 | tf_op jit(solution)/shard_map/all_gather | solution.py:72
  77.1 34.3 %collective-permute-done.1 = bf16[512,2048]{1,0:T(8,128)(2,1)} collective-permute-done((bf16[512,2048]{1,0:T(8,128)(2,1)}, bf16[512,2048]{1,0:T(8,128)(2,1)}, u32[]{:S(2)}, u32[]{:S(2)}) %collective-permute-start.1) | collective-permute-done | bytes 2097184 | tf_op jit(solution)/shard_map/ppermute | solution.py:99
  111.3 13.0 %fusion.78 = bf16[1024,2048,1]{1,0,2:T(8,128)(2,1)} fusion(s32[]{:T(128)S(6)} %select_n.26, bf16[256,2048]{1,0:T(8,128)(2,1)S(1)} %fusion.92, bf16[256,2048]{1,0:T(8,128)(2,1)S(1)} %collective-permute-done, bf16[512,2048]{1,0:T(8,128)(2,1)} %collective-permute-done.1), kind=kLoop, calls=%fused_computation.123 | loop fusion | flops 25165824 | bytes 8388612 | tf_op jit(solution)/shard_map/jit(_roll_dynamic)/dynamic_slice | solution.py:106
  124.3 10.2 %add_bitcast_fusion = f32[3,1024,512]{2,1,0:T(8,128)S(1)} fusion(f32[3,512]{1,0:T(4,128)S(1)} %bitcast.198, bf16[1024,2048,1]{1,0,2:T(8,128)(2,1)} %fusion.78, bf16[3,2048,512]{2,1,0:T(8,128)(2,1)} %all-gather.10.cloned.1.call-done), kind=kOutput, calls=%fused_computation.93 | convolution fusion | flops 6444023808 | bytes 16783360 | tf_op jit(solution)/shard_map/rd,cdk->crk/dot_general | solution.py:151
  164.1 11.5 %while.28 = (s32[]{:T(128)}, bf16[2,512,8,64]{1,3,2,0:T(8,128)(2,1)S(1)}, f32[2,8,512]{2,1,0:T(8,128)S(1)}, bf16[2,512,8,64]{1,3,2,0:T(8,128)(2,1)}, bf16[2,512,...) while((s32[]{:T(128)}, bf16[2,512,8,64]{1,3,2,0:T(8,128)(2,1)S(1)}, ...), condition=%wide.region_5.7_spmd.clone, body=%wide.region_2.6_spmd.clone.sunk | while | flops 560459776 | bytes 32639084 | solution.py:174
  188.4 10.9 %all-gather.3 = bf16[8,1,256]{2,1,0:T(2,128)(2,1)S(1)} all-gather(bf16[1,1,256]{2,1,0:T(2,128)(2,1)S(1)} %reshape.175), channel_id=1, replica_groups=mesh['dp'=8,'tensor'=4] {'dp'}, dimensions={0}, use_global_device_ids=true | all-gather | bytes 4608 | tf_op jit(solution)/shard_map/all_gather | solution.py:79
  208.1 46.7 %reduce-scatter.13.cloned.1.call-done = bf16[256,2048]{1,0:T(8,128)(2,1)} async-done(((bf16[1024,2048]{1,0:T(8,128)(2,1)}), bf16[256,2048]{1,0:T(8,128)(2,1)}) %reduce-scatter.13.cloned.1.call-update) | async-done | bytes 1048592 | tf_op jit(solution)/shard_map/reduce_scatter | solution.py:112
  263.7 19.9 %collective-permute-done.2 = bf16[256,2048]{1,0:T(8,128)(2,1)S(1)} collective-permute-done((bf16[256,2048]{1,0:T(8,128)(2,1)S(1)}, bf16[256,2048]{1,0:T(8,128)(2,1)S(1)}, u32[]{:S(2)}, u32[]{:S(2)}) %collective-permute-start.2) | collective-permute-done | bytes 1048608 | tf_op jit(solution)/shard_map/ppermute | solution.py:99
  285.3 25.4 %collective-permute-done.5 = bf16[512,2048]{1,0:T(8,128)(2,1)S(1)} collective-permute-done((bf16[512,2048]{1,0:T(8,128)(2,1)S(1)}, bf16[512,2048]{1,0:T(8,128)(2,1)S(1)}, u32[]{:S(2)}, u32[]{:S(2)}) %collective-permute-start.5) | collective-permute-done | bytes 2097184 | tf_op jit(solution)/shard_map/ppermute | solution.py:99
  310.7 43.4 %collective-permute-done.3 = bf16[512,2048]{1,0:T(8,128)(2,1)S(1)} collective-permute-done((bf16[512,2048]{1,0:T(8,128)(2,1)S(1)}, bf16[512,2048]{1,0:T(8,128)(2,1)S(1)}, u32[]{:S(2)}, u32[]{:S(2)}) %collective-permute-start.3) | collective-permute-done | bytes 2097184 | tf_op jit(solution)/shard_map/ppermute | solution.py:99
  354.1 23.2 %fusion.67 = (bf16[1024,2048]{1,0:T(8,128)(2,1)}, bf16[1024,2048]{1,0:T(8,128)(2,1)}) fusion(s32[]{:T(128)S(6)} %select_n.26, bf16[256,2048]{1,0:T(8,128)(2,1)} %param.27, bf16[256,2048]{1,0:T(8,128)(2,1)} %collective-permute-done.4, bf16[512,2048]{1,0:T(8,128)(2,1)S(1)} %collective-permute-done.5, bf16[512,2048]{1,0:T(8,128)(2,1)S(1)} %collective-permute-done.3, ...), kind=kLoop, calls=%fused_computation.112 | loop fusion | flops 50331648 | bytes 16777220 | tf_op jit(solution)/shard_map/jit(_roll_dynamic)/concatenate | solution.py:106
  377.3 11.9 %fusion.57 = f32[1024,1408]{1,0:T(8,128)} fusion(bf16[1024,2048]{1,0:T(8,128)(2,1)} %get-tuple-element.330, bf16[2,2048,1408]{2,1,0:T(8,128)(2,1)} %all-gather.14.cloned.1.call-done), kind=kOutput, calls=%fused_computation.102 | convolution fusion | flops 5905580032 | bytes 15728640 | tf_op jit(solution)/shard_map/dot_general | solution.py:189
  397.7 27.3 %all-gather.16.cloned.1.call-done = bf16[1408,2048]{1,0:T(8,128)(2,1)} async-done(((bf16[1408,256]{1,0:T(8,128)(2,1)}), bf16[1408,2048]{1,0:T(8,128)(2,1)}) %all-gather.16.cloned.1.call-update) | async-done | bytes 5767184 | tf_op jit(solution)/shard_map/all_gather | solution.py:82
  425.0 16.9 %multiply_convert_fusion.1 = (bf16[1024,1408]{1,0:T(8,128)(2,1)}, bf16[1024,1408]{1,0:T(8,128)(2,1)}, bf16[1024,1408]{1,0:T(8,128)(2,1)}) fusion(f32[1024,1408]{1,0:T(8,128)} %fusion.57, f32[1024,1408]{1,0:T(8,128)} %fusion.59, bf16[1024,2048]{1,0:T(8,128)(2,1)} %get-tuple-element.329, bf16[1408,2048]{1,0:T(8,128)(2,1)} %all-gather.16.cloned.1.call-done), kind=kOutput, calls=%fused_computation.96 | convolution fusion | flops 5927206912 | bytes 30146560 | tf_op jit(solution)/shard_map/dot_general | solution.py:203
  461.9 10.5 %convolution_convert_fusion = bf16[1408,2048]{1,0:T(8,128)(2,1)} fusion(bf16[1024,1408]{1,0:T(8,128)(2,1)} %get-tuple-element.310, bf16[1024,2048]{1,0:T(8,128)(2,1)} %get-tuple-element.329), kind=kOutput, calls=%fused_computation.89 | convolution fusion | flops 5908463616 | bytes 12845056 | tf_op jit(solution)/shard_map/dot_general | solution.py:210
  472.4 11.6 %convolution_convert_fusion.2 = bf16[2048,1408]{1,0:T(8,128)(2,1)} fusion(bf16[1024,2048]{1,0:T(8,128)(2,1)} %get-tuple-element.330, bf16[1024,1408]{1,0:T(8,128)(2,1)} %get-tuple-element.309), kind=kOutput, calls=%fused_computation.91 | convolution fusion | flops 5908463616 | bytes 12845056 | tf_op jit(solution)/shard_map/dot_general | solution.py:213
  484.1 28.7 %reduce-scatter.17.cloned.1.call-done = bf16[256,2048]{1,0:T(8,128)(2,1)} async-done(((bf16[1024,2048]{1,0:T(8,128)(2,1)}), bf16[256,2048]{1,0:T(8,128)(2,1)}) %reduce-scatter.17.cloned.1.call-update) | async-done | bytes 1048592 | tf_op jit(solution)/shard_map/reduce_scatter | solution.py:112
  529.6 14.8 %collective-permute-done.6 = bf16[256,2048]{1,0:T(8,128)(2,1)S(1)} collective-permute-done((bf16[256,2048]{1,0:T(8,128)(2,1)}, bf16[256,2048]{1,0:T(8,128)(2,1)S(1)}, u32[]{:S(2)}, u32[]{:S(2)}) %collective-permute-start.6) | collective-permute-done | bytes 1048608 | tf_op jit(solution)/shard_map/ppermute | solution.py:99
  548.7 45.2 %collective-permute-done.7 = bf16[512,2048]{1,0:T(8,128)(2,1)} collective-permute-done((bf16[512,2048]{1,0:T(8,128)(2,1)}, bf16[512,2048]{1,0:T(8,128)(2,1)}, u32[]{:S(2)}, u32[]{:S(2)}) %collective-permute-start.7) | collective-permute-done | bytes 2097184 | tf_op jit(solution)/shard_map/ppermute | solution.py:99
  593.9 10.8 %fusion.62 = bf16[1024,2048]{1,0:T(8,128)(2,1)S(1)} fusion(s32[]{:T(128)S(6)} %select_n.26, bf16[256,2048]{1,0:T(8,128)(2,1)} %fusion.107, bf16[256,2048]{1,0:T(8,128)(2,1)S(1)} %collective-permute-done.6, bf16[512,2048]{1,0:T(8,128)(2,1)} %collective-permute-done.7), kind=kLoop, calls=%fused_computation.107 | loop fusion | flops 25165824 | bytes 8388612 | tf_op jit(solution)/shard_map/jit(_roll_dynamic)/concatenate | solution.py:106
  613.7 42.8 %while.29 = (s32[]{:T(128)}, f32[2,512,8,64]{1,3,2,0:T(8,128)}, f32[2,512,8,64]{1,3,2,0:T(8,128)}, bf16[2,512,8,64]{1,3,2,0:T(8,128)(2,1)}, bf16[2,512,8,64]{1,3...) while((s32[]{:T(128)}, f32[2,512,8,64]{1,3,2,0:T(8,128)}, ...), condition=%wide.region_14.16_spmd.clone, body=%wide.region_13.15_spmd.clone.sunk | while | flops 1366552576 | bytes 120198680 | solution.py:296
  689.1 11.1 %bitcast_convert_fusion.1 = bf16[1024,2048]{1,0:T(8,128)(2,1)} fusion(bf16[3,1024,512]{2,1,0:T(8,128)(2,1)S(1)} %constant_dynamic-update-slice_fusion, bf16[3,2048,512]{2,1,0:T(8,128)(2,1)} %all-gather.10.cloned.1.call-done), kind=kOutput, calls=%fused_computation.87 | convolution fusion | flops 6444548096 | bytes 13631488 | tf_op jit(solution)/shard_map/crk,cdk->rd/dot_general | solution.py:310
  700.3 11.0 %convolution_convert_fusion.3 = bf16[1024,2048]{1,0:T(8,128)(2,1)} fusion(bf16[1024,1408]{1,0:T(8,128)(2,1)} %get-tuple-element.310, bf16[1408,2048]{1,0:T(8,128)(2,1)} %all-gather.16.cloned.1.call-done), kind=kOutput, calls=%fused_computation.126 | convolution fusion | flops 5907677184 | bytes 12845056 | tf_op jit(solution)/shard_map/dot_general | solution.py:196
  711.4 11.0 %convert_bitcast_fusion = bf16[3,2048,512]{1,2,0:T(8,128)(2,1)} fusion(bf16[3,1024,512]{2,1,0:T(8,128)(2,1)S(1)} %constant_dynamic-update-slice_fusion, bf16[1024,2048,1]{1,0,2:T(8,128)(2,1)} %fusion.78), kind=kOutput, calls=%fused_computation.92 | convolution fusion | flops 6445596672 | bytes 13631488 | tf_op jit(solution)/shard_map/rd,crk->cdk/dot_general | solution.py:307
  730.2 12.6 %reduce-scatter.31.cloned.1.call-done = bf16[64,3]{1,0:T(8,128)(2,1)} async-done(((bf16[512,3]{1,0:T(8,128)(2,1)}), bf16[64,3]{1,0:T(8,128)(2,1)}) %reduce-scatter.31.cloned.1.call-update) | async-done | bytes 400
  744.2 35.7 %reduce-scatter.23.cloned.1.call-done = bf16[512,256]{1,0:T(8,128)(2,1)} async-done(((bf16[512,2048]{1,0:T(8,128)(2,1)}), bf16[512,256]{1,0:T(8,128)(2,1)}) %reduce-scatter.23.cloned.1.call-update) | async-done | bytes 262160 | tf_op jit(solution)/shard_map/reduce_scatter | solution.py:325
  781.6 52.3 %reduce-scatter.19.cloned.1.call-done = bf16[256,2048]{1,0:T(8,128)(2,1)} async-done(((bf16[1024,2048]{1,0:T(8,128)(2,1)}), bf16[256,2048]{1,0:T(8,128)(2,1)}) %reduce-scatter.19.cloned.1.call-update) | async-done | bytes 1048592 | tf_op jit(solution)/shard_map/reduce_scatter | solution.py:112
  837.5 28.4 %all-reduce.5 = (bf16[2048]{0:T(1024)(128)(2,1)S(1)}, bf16[2048]{0:T(1024)(128)(2,1)S(1)}, bf16[2048]{0:T(1024)(128)(2,1)S(1)}, bf16[2048]{0:T(1024)(128)(2,1)S(1)}) all-reduce(bf16[2048]{0:T(1024)(128)(2,1)S(1)} %get-tuple-element.260, bf16[2048]{0:T(1024)(128)(2,1)S(1)} %reduce_sum.144, ...), channel_id=6, replica_groups=mesh['dp'=8,'tensor'=4] {'dp'}, use_global_device_ids=true, to_apply=%region_19.21.clone | all-reduce | flops 8192 | bytes 32768
  875.7 14.0 %reduce-scatter.15.cloned.1.call-done = bf16[256,2048]{1,0:T(8,128)(2,1)} async-done(((bf16[1024,2048]{1,0:T(8,128)(2,1)}), bf16[256,2048]{1,0:T(8,128)(2,1)}) %reduce-scatter.15.cloned.1.call-update) | async-done | bytes 1048592 | tf_op jit(solution)/shard_map/reduce_scatter | solution.py:112
  894.4 67.2 %reduce-scatter.21.cloned.1.call-done = bf16[3,256,512]{1,2,0:T(8,128)(2,1)} async-done(((bf16[3,2048,512]{1,2,0:T(8,128)(2,1)}), bf16[3,256,512]{1,2,0:T(8,128)(2,1)}) %reduce-scatter.21.cloned.1.call-update) | async-done | bytes 786448 | tf_op jit(solution)/shard_map/reduce_scatter | solution.py:319
  (329 shorter events, 258.8 us)
Async XLA Ops:
  7.2 117.1 %all-gather.10.cloned.1.call-start = ((), (), s32[]{:S(2)}) async-start(), calls=%async_computation.10 | async-start | bytes 7077888 | tf_op jit(solution)/shard_map/all_gather | solution.py:71
  7.9 170.0 %all-gather.12.cloned.1.call-start = ((), (), s32[]{:S(2)}) async-start(), calls=%async_computation.11 | async-start | bytes 2359296 | tf_op jit(solution)/shard_map/all_gather | solution.py:73
  36.9 25.5 %collective-permute-start = (bf16[256,2048]{1,0:T(8,128)(2,1)S(1)}, bf16[256,2048]{1,0:T(8,128)(2,1)S(1)}, u32[]{:S(2)}, u32[]{:S(2)}) collective-permute-start(bf16[256,2048]{1,0:T(8,128)(2,1)S(1)} %fusion.92), channel_id=1, source_target_pairs={{0,3},{1,0},{2,1},{3,2},{4,7},{5,4},{6,5},{7,6},{8,11},{9,8},{10,9... | collective-permute-start | bytes 3145736 | tf_op jit(solution)/shard_map/ppermute | solution.py:99
  63.8 47.5 %collective-permute-start.1 = (bf16[512,2048]{1,0:T(8,128)(2,1)}, bf16[512,2048]{1,0:T(8,128)(2,1)}, u32[]{:S(2)}, u32[]{:S(2)}) collective-permute-start(bf16[512,2048]{1,0:T(8,128)(2,1)} %pad_maximum_fusion), channel_id=1, source_target_pairs={{0,2},{1,3},{2,0},{3,1},{4,6},{5,7},{6,4},{7,5},{8,10},{9,11},{10,... | collective-permute-start | bytes 6291464 | tf_op jit(solution)/shard_map/ppermute | solution.py:99
  65.3 189.6 %reduce-scatter.13.cloned.1.call-start = ((), (), s32[]{:S(2)}) async-start(), calls=%async_computation.12 | async-start | bytes 5242880 | tf_op jit(solution)/shard_map/reduce_scatter | solution.py:112
  184.3 193.0 %all-gather.14.cloned.1.call-start = ((), (), s32[]{:S(2)}) async-start(), calls=%async_computation.13 | async-start | bytes 12976128 | tf_op jit(solution)/shard_map/all_gather | solution.py:81
  184.9 240.1 %all-gather.16.cloned.1.call-start = ((), (), s32[]{:S(2)}) async-start(), calls=%async_computation.14 | async-start | bytes 6488064 | tf_op jit(solution)/shard_map/all_gather | solution.py:82
  184.9 75.4 %collective-permute-start.4 = (bf16[256,2048]{1,0:T(8,128)(2,1)}, bf16[256,2048]{1,0:T(8,128)(2,1)}, u32[]{:S(2)}, u32[]{:S(2)}) collective-permute-start(bf16[256,2048]{1,0:T(8,128)(2,1)} %param.27), channel_id=1, source_target_pairs={{0,3},{1,0},{2,1},{3,2},{4,7},{5,4},{6,5},{7,6},{8,11},{9,8},{10,9... | collective-permute-start | bytes 3145736 | tf_op jit(solution)/shard_map/ppermute | solution.py:99
  188.3 324.4 %reduce-scatter.17.cloned.1.call-start = ((), (), s32[]{:S(2)}) async-start(), calls=%async_computation.16 | async-start | bytes 5242880 | tf_op jit(solution)/shard_map/reduce_scatter | solution.py:112
  199.3 316.5 %copy-start.27 = (f32[8,1,256]{2,1,0:T(1,128)}, f32[8,1,256]{2,1,0:T(1,128)S(1)}, u32[]{:S(2)}) copy-start(f32[8,1,256]{2,1,0:T(1,128)S(1)} %convert_element_type.191) | copy-start | bytes 24580
  256.5 259.3 %copy-start.35 = (f32[256]{0:T(256)}, f32[256]{0:T(256)S(1)}, u32[]{:S(2)}) copy-start(f32[256]{0:T(256)S(1)} %broadcast_multiply_fusion.4) | copy-start | bytes 3076
  258.3 257.5 %copy-start.39 = (f32[256]{0:T(256)}, f32[256]{0:T(256)S(1)}, u32[]{:S(2)}) copy-start(f32[256]{0:T(256)S(1)} %add_rsqrt_fusion) | copy-start | bytes 3076
  258.8 24.8 %collective-permute-start.2 = (bf16[256,2048]{1,0:T(8,128)(2,1)S(1)}, bf16[256,2048]{1,0:T(8,128)(2,1)S(1)}, u32[]{:S(2)}, u32[]{:S(2)}) collective-permute-start(bf16[256,2048]{1,0:T(8,128)(2,1)S(1)} %add_convert_fusion.2), channel_id=1, source_target_pairs={{0,3},{1,0},{2,1},{3,2},{4,7},{5,4},{6,5},{7,6},{8,11},{9,8},{10,9... | collective-permute-start | bytes 3145736 | tf_op jit(solution)/shard_map/ppermute | solution.py:99
  262.2 48.6 %collective-permute-start.5 = (bf16[512,2048]{1,0:T(8,128)(2,1)S(1)}, bf16[512,2048]{1,0:T(8,128)(2,1)S(1)}, u32[]{:S(2)}, u32[]{:S(2)}) collective-permute-start(bf16[512,2048]{1,0:T(8,128)(2,1)S(1)} %pad_maximum_fusion.2), channel_id=1, source_target_pairs={{0,2},{1,3},{2,0},{3,1},{4,6},{5,7},{6,4},{7,5},{8,10},{9,11},{10,... | collective-permute-start | bytes 6291464 | tf_op jit(solution)/shard_map/ppermute | solution.py:99
  283.8 70.3 %collective-permute-start.3 = (bf16[512,2048]{1,0:T(8,128)(2,1)S(1)}, bf16[512,2048]{1,0:T(8,128)(2,1)S(1)}, u32[]{:S(2)}, u32[]{:S(2)}) collective-permute-start(bf16[512,2048]{1,0:T(8,128)(2,1)S(1)} %pad_maximum_fusion.1), channel_id=1, source_target_pairs={{0,2},{1,3},{2,0},{3,1},{4,6},{5,7},{6,4},{7,5},{8,10},{9,11},{10,... | collective-permute-start | bytes 6291464 | tf_op jit(solution)/shard_map/ppermute | solution.py:99
  461.8 262.7 %reduce-scatter.29.cloned.1.call-start = ((), (), s32[]{:S(2)}) async-start(), calls=%async_computation.22 | async-start | bytes 6488064 | tf_op jit(solution)/shard_map/reduce_scatter | solution.py:245
  472.4 254.6 %reduce-scatter.25.cloned.1.call-start = ((), (), s32[]{:S(2)}) async-start(), calls=%async_computation.20 | async-start | bytes 6488064 | tf_op jit(solution)/shard_map/reduce_scatter | solution.py:239
  484.0 243.0 %reduce-scatter.27.cloned.1.call-start = ((), (), s32[]{:S(2)}) async-start(), calls=%async_computation.21 | async-start | bytes 6488064 | tf_op jit(solution)/shard_map/reduce_scatter | solution.py:242
  519.5 24.9 %collective-permute-start.6 = (bf16[256,2048]{1,0:T(8,128)(2,1)}, bf16[256,2048]{1,0:T(8,128)(2,1)S(1)}, u32[]{:S(2)}, u32[]{:S(2)}) collective-permute-start(bf16[256,2048]{1,0:T(8,128)(2,1)} %fusion.107), channel_id=1, source_target_pairs={{0,3},{1,0},{2,1},{3,2},{4,7},{5,4},{6,5},{7,6},{8,11},{9,8},{10,9... | collective-permute-start | bytes 3145736 | tf_op jit(solution)/shard_map/ppermute | solution.py:99
  529.6 213.2 %reduce-scatter.31.cloned.1.call-start = ((), (), s32[]{:S(2)}) async-start(), calls=%async_computation.23 | async-start | bytes 147456
  547.2 46.7 %collective-permute-start.7 = (bf16[512,2048]{1,0:T(8,128)(2,1)}, bf16[512,2048]{1,0:T(8,128)(2,1)}, u32[]{:S(2)}, u32[]{:S(2)}) collective-permute-start(bf16[512,2048]{1,0:T(8,128)(2,1)} %pad_maximum_fusion.3), channel_id=1, source_target_pairs={{0,2},{1,3},{2,0},{3,1},{4,6},{5,7},{6,4},{7,5},{8,10},{9,11},{10,... | collective-permute-start | bytes 6291464 | tf_op jit(solution)/shard_map/ppermute | solution.py:99
  682.8 97.1 %reduce-scatter.23.cloned.1.call-start = ((), (), s32[]{:S(2)}) async-start(), calls=%async_computation.19 | async-start | bytes 2359296 | tf_op jit(solution)/shard_map/reduce_scatter | solution.py:325
  689.1 144.8 %reduce-scatter.19.cloned.1.call-start = ((), (), s32[]{:S(2)}) async-start(), calls=%async_computation.17 | async-start | bytes 5242880 | tf_op jit(solution)/shard_map/reduce_scatter | solution.py:112
  700.3 189.4 %reduce-scatter.15.cloned.1.call-start = ((), (), s32[]{:S(2)}) async-start(), calls=%async_computation.15 | async-start | bytes 5242880 | tf_op jit(solution)/shard_map/reduce_scatter | solution.py:112
  711.4 250.2 %reduce-scatter.21.cloned.1.call-start = ((), (), s32[]{:S(2)}) async-start(), calls=%async_computation.18 | async-start | bytes 7077888 | tf_op jit(solution)/shard_map/reduce_scatter | solution.py:319
  724.5 110.8 %copy-start.1 = (bf16[256,2048]{1,0:T(8,128)(2,1)S(1)}, bf16[256,2048]{1,0:T(8,128)(2,1)}, u32[]{:S(2)}) copy-start(bf16[256,2048]{1,0:T(8,128)(2,1)} %param.17) | copy-start | bytes 3145732
  727.0 162.7 %copy-start.7 = (bf16[256,2048]{1,0:T(8,128)(2,1)S(1)}, bf16[256,2048]{1,0:T(8,128)(2,1)}, u32[]{:S(2)}) copy-start(bf16[256,2048]{1,0:T(8,128)(2,1)} %reduce-scatter.13.cloned.1.call-done) | copy-start | bytes 3145732
  727.0 162.7 %copy-start.28 = (f32[8,1,256]{2,1,0:T(1,128)S(1)}, f32[8,1,256]{2,1,0:T(1,128)}, u32[]{:S(2)}) copy-start(f32[8,1,256]{2,1,0:T(1,128)} %copy-done.27) | copy-start | bytes 24580
  727.0 162.7 %copy-start.36 = (f32[256]{0:T(256)S(1)}, f32[256]{0:T(256)}, u32[]{:S(2)}) copy-start(f32[256]{0:T(256)} %copy-done.35) | copy-start | bytes 3076
  727.0 162.7 %copy-start.40 = (f32[256]{0:T(256)S(1)}, f32[256]{0:T(256)}, u32[]{:S(2)}) copy-start(f32[256]{0:T(256)} %copy-done.39) | copy-start | bytes 3076
  727.0 162.7 %copy-start.45 = (f32[256]{0:T(256)S(1)}, f32[256]{0:T(256)}, u32[]{:S(2)}) copy-start(f32[256]{0:T(256)} %copy-done.44) | copy-start | bytes 3076
  727.0 162.7 %copy-start.47 = (f32[256]{0:T(256)S(1)}, f32[256]{0:T(256)}, u32[]{:S(2)}) copy-start(f32[256]{0:T(256)} %copy-done.46) | copy-start | bytes 3076
  (63 other events, 1038.5 us)
Sparse Core Ops, SparseCore 0:
  9.6 67.4 all-gather.9
  78.7 29.2 all-gather.11
  184.4 70.3 reduce-scatter.12
  256.3 108.0 all-gather.13
  365.8 59.0 all-gather.15
  461.9 50.7 reduce-scatter.16
  515.1 64.7 reduce-scatter.28
  582.2 63.2 reduce-scatter.24
  647.8 63.2 reduce-scatter.26
  713.7 29.0 reduce-scatter.30
  745.7 34.1 reduce-scatter.22
  782.7 51.1 reduce-scatter.18
  836.9 52.7 reduce-scatter.14
  891.8 69.7 reduce-scatter.20
